TPU v7x, 128 devices: a whole 4x4x4 slice. The times are simulated.
128 devices in a mesh: slab: 64 (over y, z, x), blk: 2 (over core).
Axes of the slice: x: 4, y: 4, z: 4, core: 2. Of those that a mesh axis runs over, the one named last changes fastest.
Arguments:
- p_blocks: bfloat16 [2, 2048, 64, 64], P('blk', 'slab'), may hold values from -0.75 to 0.75
- basis_vals: bfloat16 [512, 8, 64, 128], P('slab'), may hold values from -0.75 to 0.75
- need_list: int32 [2, 64, 64, 4], P('blk', 'slab'), may hold values from 0 to 31, as said below
- tasks: int32 [2, 64, 4, 1536], P('blk', 'slab'), may hold values from 0 to 255, as said below
- task_counts: int32 [2, 64], P('blk', 'slab'), may hold values from 1 to 1536, as said below
Outputs:
- density: float32 [512, 128], P('slab')
- potential_blocks: float32 [2, 2048, 64, 64], P('blk', 'slab')
Inputs may be any that keep to these rules, and one draw needn't show every extreme that they name: The 4 entries of one need_list[c, s, o, :] are distinct. `tasks`: field 0 is below 8, fields 1 and 2 below 8, field 3 below 256. `task_counts`: some device has 1536 live tasks.
All inputs are finite; a program needn't handle non-finite values.
Results may differ from a plain program's by a relative error of at most 0.0029.
Values may be sent and summed in bfloat16 or wider, within the bound.
No kernel may reach another device: no remote copies, remote signals or barrier semaphores. Data moves between devices by JAX's collectives and lax.ppermute only.
A program may use at most 128 MiB of HBM per device.

v0:
```python
import jax
import jax.numpy as jnp
from jax import lax
from jax.sharding import PartitionSpec as P


def body(p_blocks, basis_vals, need_list, tasks, task_counts):
    slabs = lax.axis_size("slab")
    owned_blocks = p_blocks[0]
    blk_dev = owned_blocks.shape[0]
    block_size = owned_blocks.shape[1]
    wanted_ids = need_list[0, 0]
    capacity = wanted_ids.shape[1]
    requested = lax.all_to_all(wanted_ids, "slab", split_axis=0, concat_axis=0, tiled=True)
    column_all = lax.all_gather(owned_blocks, "slab", axis=0, tiled=True)
    offsets = jnp.arange(slabs, dtype=jnp.int32)[:, None] * blk_dev
    global_ids = (offsets + wanted_ids).reshape(-1)
    received = column_all[global_ids]
    task_fields = tasks[0, 0]
    live_count = task_counts[0, 0]
    nbat_local = basis_vals.shape[0]
    grid_coordinates = basis_vals.shape[3]
    task_slots = task_fields.shape[1]
    tile_rows = min(256, task_slots)
    tile_count = task_slots // tile_rows
    batch_range = jnp.arange(nbat_local, dtype=jnp.int32)

    def tile_terms(tile_index):
        fields_tile = lax.dynamic_slice_in_dim(task_fields, tile_index * tile_rows, tile_rows, 1)
        grid_batch_index = fields_tile[0]
        live_mask = (
            tile_index * tile_rows + jnp.arange(tile_rows, dtype=jnp.int32) < live_count
        ).astype(jnp.float32)
        left_vals = basis_vals[grid_batch_index, fields_tile[1]]
        right_side_values = basis_vals[grid_batch_index, fields_tile[2]]
        return (grid_batch_index, fields_tile[3], live_mask, left_vals, right_side_values)

    def density_tile(total, tile_index):
        grid_batch_index, slot_ids, live_mask, left_vals, right_side_values = tile_terms(tile_index)
        selected_entries = received[slot_ids]
        mapped_result = jnp.einsum(
            "zhf,zfx->zhx", selected_entries, right_side_values, preferred_element_type=jnp.float32
        )
        contrib = (
            jnp.sum(left_vals.astype(jnp.float32) * mapped_result, axis=1) * live_mask[:, None]
        )
        one_hot = (grid_batch_index[:, None] == batch_range[None, :]).astype(jnp.float32)
        added = jnp.dot(
            one_hot.T, contrib, precision=lax.Precision.HIGHEST, preferred_element_type=jnp.float32
        )
        return (total + added, None)

    tile_ids = jnp.arange(tile_count, dtype=jnp.int32)
    partial_density, _ = lax.scan(
        density_tile, jnp.zeros((nbat_local, grid_coordinates), jnp.float32), tile_ids
    )
    density = lax.psum(partial_density, "blk")
    potential = density / jnp.sqrt(1.0 + density * density)

    def potential_tile(slot_sums, tile_index):
        grid_batch_index, slot_ids, live_mask, left_vals, right_side_values = tile_terms(tile_index)
        weight_applied = (
            left_vals.astype(jnp.float32) * potential[grid_batch_index][:, None, :]
        ).astype(jnp.bfloat16)
        incomplete_sum_terms = jnp.einsum(
            "lkf,lgf->lkg", weight_applied, right_side_values, preferred_element_type=jnp.float32
        )
        incomplete_sum_terms = incomplete_sum_terms * live_mask[:, None, None]
        return (slot_sums.at[slot_ids].add(incomplete_sum_terms), None)

    slot_start = jnp.zeros((slabs * capacity, block_size, block_size), jnp.float32)
    slot_sums, _ = lax.scan(potential_tile, slot_start, tile_ids)
    returned = lax.all_to_all(
        slot_sums.reshape(slabs, capacity, block_size, block_size),
        "slab",
        split_axis=0,
        concat_axis=0,
        tiled=True,
    )
    owner_sums = jnp.zeros((blk_dev, block_size, block_size), jnp.float32)
    owner_sums = owner_sums.at[requested.reshape(-1)].add(
        returned.reshape(slabs * capacity, block_size, block_size)
    )
    return (density, owner_sums[None])


def solution(mesh):
    in_specs = (
        P("blk", "slab", None, None),
        P("slab", None, None, None),
        P("blk", "slab", None, None),
        P("blk", "slab", None, None),
        P("blk", "slab"),
    )
    out_specs = (P("slab", None), P("blk", "slab", None, None))
    return jax.shard_map(body, mesh=mesh, in_specs=in_specs, out_specs=out_specs, check_vma=False)
```

profile of v0, /device:TPU:0, one launch (start us, length us, event | category | flops | bytes accessed | tf_op | source)
XLA Modules:
  0.0 798.4 jit_solution(16260203998572006986)
XLA Ops:
  9.3 11.5 %all-to-all-start = ((s32[64,1,4]{2,1,0:T(1,128)}), s32[64,1,4]{2,1,0:T(1,128)S(1)}, u32[]{:S(2)}, u32[]{:S(2)}) async-start(s32[64,1,4]{2,1,0:T(1,128)} %bitcast.14), calls=%async_computation | async-start | bytes 65536 | tf_op jit(solution)/shard_map/all_to_all | solution.py:14
  21.9 152.0 %all-gather.3.cloned.1.call-done = bf16[1,2048,64,64]{3,2,0,1:T(8,128)(2,1)} async-done(((bf16[1,32,64,64]{3,2,0,1:T(8,128)(2,1)}), bf16[1,2048,64,64]{3,2,0,1:T(8,128)(2,1)}) %all-gather.3.cloned.1.call-update) | async-done | bytes 16777232 | tf_op jit(solution)/shard_map/all_gather | solution.py:15
  174.0 5.0 gather_fusion.6
  179.0 130.2 %while.22 = (s32[]{:T(128)}, f32[8,128]{1,0:T(8,128)S(1)}, s32[6]{0:T(128)S(1)}, s32[4,1536]{1,0:T(4,128)}, bf16[8,8,64,128]{3,2,1,0:T(8,128)(2,1)S(1)}, /*index...) while((s32[]{:T(128)}, f32[8,128]{1,0:T(8,128)S(1)}, ...), condition=%wide.region_2.3_spmd.clone, body=%wide.region_0.2_spmd.clone.sunk | while | flops 277883648 | bytes 31750408 | solution.py:54
  184.5 3.4 gather_fusion.5
  187.8 5.2 gather_fusion.4
  193.1 5.9 multiply_reduce_fusion.2
  206.2 3.4 gather_fusion.5
  209.5 5.2 gather_fusion.4
  214.8 5.9 multiply_reduce_fusion.2
  227.9 3.4 gather_fusion.5
  231.2 5.2 gather_fusion.4
  236.5 5.9 multiply_reduce_fusion.2
  249.6 3.4 gather_fusion.5
  253.0 5.2 gather_fusion.4
  258.2 5.9 multiply_reduce_fusion.2
  271.3 3.4 gather_fusion.5
  274.7 5.2 gather_fusion.4
  279.9 5.9 multiply_reduce_fusion.2
  293.0 3.4 gather_fusion.5
  296.4 5.2 gather_fusion.4
  301.6 5.9 multiply_reduce_fusion.2
  311.7 4.3 broadcast_in_dim.10
  316.0 352.7 %while.21 = (s32[]{:T(128)}, f32[256,64,64]{2,1,0:T(8,128)}, s32[6]{0:T(128)S(1)}, s32[4,1536]{1,0:T(4,128)}, bf16[8,8,64,128]{3,2,1,0:T(8,128)(2,1)S(1)}, /*ind...) while((s32[]{:T(128)}, f32[256,64,64]{2,1,0:T(8,128)}, ...), condition=%wide.region_6.7_spmd, body=%wide.region_4.6_spmd.sunk | while | flops 276830976 | bytes 42358008 | solution.py:72
  321.6 3.4 gather_fusion.1
  326.3 9.0 %broadcast_multiply_fusion.2 = f32[256,64,64]{2,1,0:T(8,128)} fusion(f32[256]{0:T(256)S(1)} %compare_convert_fusion.4, bf16[256,64,128]{2,1,0:T(8,128)(2,1)} %gather_fusion, bf16[256,64,128]{2,1,0:T(8,128)(2,1)} %gather_fusion.1, f32[256,128]{1,0:T(8,128)S(1)} %gather_fusion.2), kind=kOutput, calls=%fused_computation.12.clone.1 | convolution fusion | flops 275775488 | bytes 12715008 | tf_op jit(solution)/shard_map/while/body/eval_jaxpr/lkf,lgf->lkg/dot_general | solution.py:65
  335.4 39.4 %scatter_fusion = f32[256,64,64]{2,1,0:T(8,128)} fusion(f32[256,64,64]{2,1,0:T(8,128)} %get-tuple-element.301, s32[256]{0:T(256)S(1)} %bitcast.104, f32[256,64,64]{2,1,0:T(8,128)} %broadcast_multiply_fusion.2), kind=kCustom, calls=%fused_computation.7.clone.1 | custom fusion | flops 1048576 | bytes 12583936 | tf_op jit(solution)/shard_map/while/body/eval_jaxpr/scatter-add | solution.py:69
  380.4 3.4 gather_fusion.1
  385.1 9.0 %broadcast_multiply_fusion.2 = f32[256,64,64]{2,1,0:T(8,128)} fusion(f32[256]{0:T(256)S(1)} %compare_convert_fusion.4, bf16[256,64,128]{2,1,0:T(8,128)(2,1)} %gather_fusion, bf16[256,64,128]{2,1,0:T(8,128)(2,1)} %gather_fusion.1, f32[256,128]{1,0:T(8,128)S(1)} %gather_fusion.2), kind=kOutput, calls=%fused_computation.12.clone.1 | convolution fusion | flops 275775488 | bytes 12715008 | tf_op jit(solution)/shard_map/while/body/eval_jaxpr/lkf,lgf->lkg/dot_general | solution.py:65
  394.1 39.5 %scatter_fusion = f32[256,64,64]{2,1,0:T(8,128)} fusion(f32[256,64,64]{2,1,0:T(8,128)} %get-tuple-element.301, s32[256]{0:T(256)S(1)} %bitcast.104, f32[256,64,64]{2,1,0:T(8,128)} %broadcast_multiply_fusion.2), kind=kCustom, calls=%fused_computation.7.clone.1 | custom fusion | flops 1048576 | bytes 12583936 | tf_op jit(solution)/shard_map/while/body/eval_jaxpr/scatter-add | solution.py:69
  439.2 3.4 gather_fusion.1
  443.9 9.0 %broadcast_multiply_fusion.2 = f32[256,64,64]{2,1,0:T(8,128)} fusion(f32[256]{0:T(256)S(1)} %compare_convert_fusion.4, bf16[256,64,128]{2,1,0:T(8,128)(2,1)} %gather_fusion, bf16[256,64,128]{2,1,0:T(8,128)(2,1)} %gather_fusion.1, f32[256,128]{1,0:T(8,128)S(1)} %gather_fusion.2), kind=kOutput, calls=%fused_computation.12.clone.1 | convolution fusion | flops 275775488 | bytes 12715008 | tf_op jit(solution)/shard_map/while/body/eval_jaxpr/lkf,lgf->lkg/dot_general | solution.py:65
  453.0 39.4 %scatter_fusion = f32[256,64,64]{2,1,0:T(8,128)} fusion(f32[256,64,64]{2,1,0:T(8,128)} %get-tuple-element.301, s32[256]{0:T(256)S(1)} %bitcast.104, f32[256,64,64]{2,1,0:T(8,128)} %broadcast_multiply_fusion.2), kind=kCustom, calls=%fused_computation.7.clone.1 | custom fusion | flops 1048576 | bytes 12583936 | tf_op jit(solution)/shard_map/while/body/eval_jaxpr/scatter-add | solution.py:69
  498.0 3.4 gather_fusion.1
  502.8 9.0 %broadcast_multiply_fusion.2 = f32[256,64,64]{2,1,0:T(8,128)} fusion(f32[256]{0:T(256)S(1)} %compare_convert_fusion.4, bf16[256,64,128]{2,1,0:T(8,128)(2,1)} %gather_fusion, bf16[256,64,128]{2,1,0:T(8,128)(2,1)} %gather_fusion.1, f32[256,128]{1,0:T(8,128)S(1)} %gather_fusion.2), kind=kOutput, calls=%fused_computation.12.clone.1 | convolution fusion | flops 275775488 | bytes 12715008 | tf_op jit(solution)/shard_map/while/body/eval_jaxpr/lkf,lgf->lkg/dot_general | solution.py:65
  511.8 39.3 %scatter_fusion = f32[256,64,64]{2,1,0:T(8,128)} fusion(f32[256,64,64]{2,1,0:T(8,128)} %get-tuple-element.301, s32[256]{0:T(256)S(1)} %bitcast.104, f32[256,64,64]{2,1,0:T(8,128)} %broadcast_multiply_fusion.2), kind=kCustom, calls=%fused_computation.7.clone.1 | custom fusion | flops 1048576 | bytes 12583936 | tf_op jit(solution)/shard_map/while/body/eval_jaxpr/scatter-add | solution.py:69
  556.7 3.4 gather_fusion.1
  561.4 9.0 %broadcast_multiply_fusion.2 = f32[256,64,64]{2,1,0:T(8,128)} fusion(f32[256]{0:T(256)S(1)} %compare_convert_fusion.4, bf16[256,64,128]{2,1,0:T(8,128)(2,1)} %gather_fusion, bf16[256,64,128]{2,1,0:T(8,128)(2,1)} %gather_fusion.1, f32[256,128]{1,0:T(8,128)S(1)} %gather_fusion.2), kind=kOutput, calls=%fused_computation.12.clone.1 | convolution fusion | flops 275775488 | bytes 12715008 | tf_op jit(solution)/shard_map/while/body/eval_jaxpr/lkf,lgf->lkg/dot_general | solution.py:65
  570.5 39.4 %scatter_fusion = f32[256,64,64]{2,1,0:T(8,128)} fusion(f32[256,64,64]{2,1,0:T(8,128)} %get-tuple-element.301, s32[256]{0:T(256)S(1)} %bitcast.104, f32[256,64,64]{2,1,0:T(8,128)} %broadcast_multiply_fusion.2), kind=kCustom, calls=%fused_computation.7.clone.1 | custom fusion | flops 1048576 | bytes 12583936 | tf_op jit(solution)/shard_map/while/body/eval_jaxpr/scatter-add | solution.py:69
  615.4 3.4 gather_fusion.1
  620.2 9.0 %broadcast_multiply_fusion.2 = f32[256,64,64]{2,1,0:T(8,128)} fusion(f32[256]{0:T(256)S(1)} %compare_convert_fusion.4, bf16[256,64,128]{2,1,0:T(8,128)(2,1)} %gather_fusion, bf16[256,64,128]{2,1,0:T(8,128)(2,1)} %gather_fusion.1, f32[256,128]{1,0:T(8,128)S(1)} %gather_fusion.2), kind=kOutput, calls=%fused_computation.12.clone.1 | convolution fusion | flops 275775488 | bytes 12715008 | tf_op jit(solution)/shard_map/while/body/eval_jaxpr/lkf,lgf->lkg/dot_general | solution.py:65
  629.2 39.5 %scatter_fusion = f32[256,64,64]{2,1,0:T(8,128)} fusion(f32[256,64,64]{2,1,0:T(8,128)} %get-tuple-element.301, s32[256]{0:T(256)S(1)} %bitcast.104, f32[256,64,64]{2,1,0:T(8,128)} %broadcast_multiply_fusion.2), kind=kCustom, calls=%fused_computation.7.clone.1 | custom fusion | flops 1048576 | bytes 12583936 | tf_op jit(solution)/shard_map/while/body/eval_jaxpr/scatter-add | solution.py:69
  668.7 9.7 %reshape.408 = f32[64,1,16384]{2,1,0:T(1,128)} reshape(f32[64,4,64,64]{3,2,1,0:T(8,128)} %bitcast.99) | data formatting | bytes 8388608
  678.4 9.1 %all-to-all-start.1 = ((f32[64,1,16384]{2,1,0:T(1,128)}), f32[64,1,16384]{2,1,0:T(1,128)}, u32[]{:S(2)}, u32[]{:S(2)}) async-start(f32[64,1,16384]{2,1,0:T(1,128)} %reshape.408), calls=%async_computation.1 | async-start | bytes 8388608 | tf_op jit(solution)/shard_map/all_to_all | solution.py:73
  688.9 53.8 %all-to-all-done.1 = f32[64,1,16384]{2,1,0:T(1,128)} async-done(((f32[64,1,16384]{2,1,0:T(1,128)}), f32[64,1,16384]{2,1,0:T(1,128)}, u32[]{:S(2)}, u32[]{:S(2)}) %all-to-all-start.1) | async-done | bytes 4194336 | tf_op jit(solution)/shard_map/all_to_all | solution.py:73
  743.2 13.7 %reduce.4 = f32[64,16384]{1,0:T(8,128)} reduce(f32[64,1,16384]{2,1,0:T(1,128)} %all-to-all-done.1, f32[]{:T(128)} %broadcast.330), dimensions={1}, to_apply=%all_to_all.11.reduce_sub_computation | reduce | bytes 8388612 | tf_op jit(solution)/shard_map/all_to_all | solution.py:73
  757.0 7.4 reshape.409
  764.4 26.1 %scatter_fusion.1 = f32[32,64,64]{2,1,0:T(8,128)S(1)} fusion(f32[32,64,64]{2,1,0:T(8,128)S(1)} %broadcast_in_dim.9, s32[256]{0:T(256)S(1)} %bitcast.109, f32[256,64,64]{2,1,0:T(8,128)} %bitcast.101), kind=kCustom, calls=%fused_computation.8 | custom fusion | flops 1048576 | bytes 12583936 | tf_op jit(solution)/shard_map/scatter-add | solution.py:81
  (105 shorter events, 85.5 us)
Async XLA Ops:
  7.2 166.8 %all-gather.3.cloned.1.call-start = ((), (), s32[]{:S(2)}) async-start(), calls=%async_computation.2 | async-start | bytes 34078720 | tf_op jit(solution)/shard_map/all_gather | solution.py:15
  9.3 669.1 %all-to-all-start = ((s32[64,1,4]{2,1,0:T(1,128)}), s32[64,1,4]{2,1,0:T(1,128)S(1)}, u32[]{:S(2)}, u32[]{:S(2)}) async-start(s32[64,1,4]{2,1,0:T(1,128)} %bitcast.14), calls=%async_computation | async-start | bytes 65536 | tf_op jit(solution)/shard_map/all_to_all | solution.py:14
  174.0 5.0 copy-start
  311.7 4.3 copy-start.2
  678.4 64.3 %all-to-all-start.1 = ((f32[64,1,16384]{2,1,0:T(1,128)}), f32[64,1,16384]{2,1,0:T(1,128)}, u32[]{:S(2)}, u32[]{:S(2)}) async-start(f32[64,1,16384]{2,1,0:T(1,128)} %reshape.408), calls=%async_computation.1 | async-start | bytes 8388608 | tf_op jit(solution)/shard_map/all_to_all | solution.py:73
  790.6 1.0 copy-start.1
Sparse Core Ops, SparseCore 0:
  10.9 163.0 all-gather.2
where the time goes:
time: 804 us; the launch traced here: 798 us
  other arithmetic  296 us (37%)
  waiting for transfers between devices  207 us (26%)
  local copies, waits for them, and re-layouts  159 us (20%)
  matrix products  91.6 us (11%)
  starting transfers between devices  20.7 us (3%)
  between operations  14.1 us (2%)
  loops' own time  8.14 us (1%)
    scatter-add x6, other arithmetic, potential_tile(): return (slot_sums.at[slot_ids].add(incomplete_sum_terms), None)  237 us
    all_gather x1, waiting for transfers between devices, body(): column_all = lax.all_gather(owned_blocks, 'slab', axis=0, tiled=True)  152 us
    dot_general x6, matrix products, potential_tile(): jnp.einsum('lkf,lgf->lkg', weight_applied, right_side_values, preferred_e...  54.1 us
    all_to_all x1, waiting for transfers between devices, body(): lax.all_to_all(slot_sums.reshape(slabs, capacity, block_size, block_size)...  53.8 us
    gather x12, local copies, waits for them, and re-layouts, tile_terms(): right_side_values = basis_vals[grid_batch_index, fields_tile[2]]  40 us
    gather x12, local copies, waits for them, and re-layouts, tile_terms(): left_vals = basis_vals[grid_batch_index, fields_tile[1]]  40 us
    dot_general x6, matrix products, density_tile(): jnp.einsum('zhf,zfx->zhx', selected_entries, right_side_values, preferred...  35.5 us
    gather x6, local copies, waits for them, and re-layouts, density_tile(): selected_entries = received[slot_ids]  31.5 us
  transfers between devices with their start and end apart: 3, of which 2 were waited for; matrix products, arithmetic and copies ran while one was open for 62% of the time, Pallas kernels for 0%

commit v1 on v0

--- a/solution.py
+++ b/solution.py
@@ -12,7 +12,9 @@
     wanted_ids = need_list[0, 0]
     capacity = wanted_ids.shape[1]
     requested = lax.all_to_all(wanted_ids, "slab", split_axis=0, concat_axis=0, tiled=True)
-    column_all = lax.all_gather(owned_blocks, "slab", axis=0, tiled=True)
+    column_all = jnp.concatenate(
+        lax.all_to_all(jnp.stack([owned_blocks] * lax.axis_size("slab")), "slab", 0, 0), axis=0
+    )
     offsets = jnp.arange(slabs, dtype=jnp.int32)[:, None] * blk_dev
     global_ids = (offsets + wanted_ids).reshape(-1)
     received = column_all[global_ids]

time: 804 us -> 1050 us (1.31)
  local copies, waits for them, and re-layouts: 159 us -> 273 us
  waiting for transfers between devices: 207 us -> 308 us
  starting transfers between devices: 20.7 us -> 63.7 us
  between operations: 14.1 us -> 0.75 us
    all_to_all x0 -> x1, waiting for transfers between devices: none -> 255 us  [body(): lax.all_to_all(jnp.stack([owned_blocks] * lax.axis_size('slab')), 'slab',...]
    all_gather x1 -> x0, waiting for transfers between devices: 152 us -> none  [body(): column_all = lax.all_gather(owned_blocks, 'slab', axis=0, tiled=True)]
    unnamed x9 -> x13, local copies, waits for them, and re-layouts: 19.4 us -> 122 us
    all_to_all x1, starting transfers between devices: 11.5 us -> 41.1 us  [body(): lax.all_to_all(wanted_ids, 'slab', split_axis=0, concat_axis=0, tiled=True)]
    another operation x0 -> x1, local copies, waits for them, and re-layouts: none -> 12 us  [body(): jnp.stack([owned_blocks] * lax.axis_size('slab'))]
    all_to_all x0 -> x1, starting transfers between devices: none -> 11.9 us  [body(): lax.all_to_all(jnp.stack([owned_blocks] * lax.axis_size('slab')), 'slab',...]
  transfers between devices with their start and end apart: 3 -> 3, of which waited for: 2 -> 2; matrix products, arithmetic and copies ran while one was open for 62% -> 53% of each run, Pallas kernels for 0% -> 0%
where the time goes in v1:
time: 1050 us; the launch traced here: 1040 us
  waiting for transfers between devices  308 us (29%)
  other arithmetic  297 us (28%)
  local copies, waits for them, and re-layouts  273 us (26%)
  matrix products  91.6 us (9%)
  starting transfers between devices  63.7 us (6%)
    all_to_all x1, waiting for transfers between devices, body(): lax.all_to_all(jnp.stack([owned_blocks] * lax.axis_size('slab')), 'slab',...  255 us
    scatter-add x6, other arithmetic, potential_tile(): return (slot_sums.at[slot_ids].add(incomplete_sum_terms), None)  237 us
    unnamed x13, local copies, waits for them, and re-layouts  122 us
    dot_general x6, matrix products, potential_tile(): jnp.einsum('lkf,lgf->lkg', weight_applied, right_side_values, preferred_e...  54.1 us
    all_to_all x1, waiting for transfers between devices, body(): lax.all_to_all(slot_sums.reshape(slabs, capacity, block_size, block_size)...  53.1 us
    all_to_all x1, starting transfers between devices, body(): lax.all_to_all(wanted_ids, 'slab', split_axis=0, concat_axis=0, tiled=True)  41.1 us
    gather x12, local copies, waits for them, and re-layouts, tile_terms(): right_side_values = basis_vals[grid_batch_index, fields_tile[2]]  40 us
    gather x12, local copies, waits for them, and re-layouts, tile_terms(): left_vals = basis_vals[grid_batch_index, fields_tile[1]]  40 us
  transfers between devices with their start and end apart: 3, of which 2 were waited for; matrix products, arithmetic and copies ran while one was open for 53% of the time, Pallas kernels for 0%

profile of v1, /device:TPU:0, one launch (start us, length us, event | category | flops | bytes accessed | tf_op | source)
XLA Modules:
  0.0 1044.2 jit_solution(17983553166799614649)
XLA Ops:
  0.6 12.0 %stack.3 = bf16[64,32,64,64]{3,2,1,0:T(8,128)(2,1)} broadcast(bf16[32,64,64]{2,1,0:T(8,128)(2,1)} %bitcast.103), dimensions={1,2,3} | broadcast | bytes 17039360 | tf_op jit(solution)/shard_map/stack | solution.py:16
  12.6 52.2 %reshape.412 = bf16[64,2,65536]{2,1,0:T(2,128)(2,1)} reshape(bf16[64,32,64,64]{3,2,1,0:T(8,128)(2,1)} %stack.3) | data formatting | bytes 33554432
  64.8 11.9 %all-to-all-start = ((bf16[64,2,65536]{2,1,0:T(2,128)(2,1)}), bf16[64,2,65536]{2,1,0:T(2,128)(2,1)}, u32[]{:S(2)}, u32[]{:S(2)}) async-start(bf16[64,2,65536]{2,1,0:T(2,128)(2,1)} %reshape.412), calls=%async_computation | async-start | bytes 33554432 | tf_op jit(solution)/shard_map/all_to_all | solution.py:16
  78.5 254.6 %all-to-all-done = bf16[64,2,65536]{2,1,0:T(2,128)(2,1)} async-done(((bf16[64,2,65536]{2,1,0:T(2,128)(2,1)}), bf16[64,2,65536]{2,1,0:T(2,128)(2,1)}, u32[]{:S(2)}, u32[]{:S(2)}) %all-to-all-start) | async-done | bytes 16777248 | tf_op jit(solution)/shard_map/all_to_all | solution.py:16
  333.1 41.1 %all-to-all-start.1 = ((s32[64,1,4]{2,1,0:T(1,128)}), s32[64,1,4]{2,1,0:T(1,128)}, u32[]{:S(2)}, u32[]{:S(2)}) async-start(s32[64,1,4]{2,1,0:T(1,128)} %bitcast.14), calls=%async_computation.1 | async-start | bytes 65536 | tf_op jit(solution)/shard_map/all_to_all | solution.py:14
  374.2 50.7 %reshape.413 = bf16[64,32,64,64]{3,2,1,0:T(8,128)(2,1)} reshape(bf16[64,2,65536]{2,1,0:T(2,128)(2,1)} %all-to-all-done) | data formatting | bytes 33554432
  424.9 5.0 gather_fusion.6
  430.0 130.2 %while.22 = (s32[]{:T(128)}, f32[8,128]{1,0:T(8,128)S(1)}, s32[6]{0:T(128)S(1)}, s32[4,1536]{1,0:T(4,128)}, bf16[8,8,64,128]{3,2,1,0:T(8,128)(2,1)S(1)}, /*index...) while((s32[]{:T(128)}, f32[8,128]{1,0:T(8,128)S(1)}, ...), condition=%wide.region_2.3_spmd.clone, body=%wide.region_0.2_spmd.clone.sunk | while | flops 277883648 | bytes 31750416 | solution.py:56
  435.4 5.2 gather_fusion.4
  440.7 3.4 gather_fusion.5
  444.1 5.9 multiply_reduce_fusion.2
  457.1 5.2 gather_fusion.4
  462.4 3.4 gather_fusion.5
  465.8 5.9 multiply_reduce_fusion.2
  478.9 5.2 gather_fusion.4
  484.1 3.4 gather_fusion.5
  487.5 5.9 multiply_reduce_fusion.2
  500.6 5.2 gather_fusion.4
  505.8 3.4 gather_fusion.5
  509.2 5.9 multiply_reduce_fusion.2
  522.3 5.2 gather_fusion.4
  527.5 3.4 gather_fusion.5
  530.9 5.9 multiply_reduce_fusion.2
  544.0 5.2 gather_fusion.4
  549.2 3.4 gather_fusion.5
  552.6 5.9 multiply_reduce_fusion.2
  562.7 4.3 broadcast_in_dim.10
  567.0 352.7 %while.21 = (s32[]{:T(128)}, f32[256,64,64]{2,1,0:T(8,128)}, s32[6]{0:T(128)S(1)}, s32[4,1536]{1,0:T(4,128)}, bf16[8,8,64,128]{3,2,1,0:T(8,128)(2,1)S(1)}, /*ind...) while((s32[]{:T(128)}, f32[256,64,64]{2,1,0:T(8,128)}, ...), condition=%wide.region_6.7_spmd, body=%wide.region_4.6_spmd.sunk | while | flops 276830976 | bytes 42358016 | solution.py:74
  573.2 3.4 gather_fusion.1
  577.3 9.0 broadcast_multiply_fusion.2
  586.3 39.4 %scatter_fusion = f32[256,64,64]{2,1,0:T(8,128)} fusion(f32[256,64,64]{2,1,0:T(8,128)} %get-tuple-element.308, s32[256]{0:T(256)S(1)} %bitcast.104, f32[256,64,64]{2,1,0:T(8,128)} %broadcast_multiply_fusion.2), kind=kCustom, calls=%fused_computation.7.clone.1 | custom fusion | flops 1048576 | bytes 12583936 | tf_op jit(solution)/shard_map/while/body/eval_jaxpr/scatter-add | solution.py:71
  632.0 3.4 gather_fusion.1
  636.1 9.0 broadcast_multiply_fusion.2
  645.1 39.5 %scatter_fusion = f32[256,64,64]{2,1,0:T(8,128)} fusion(f32[256,64,64]{2,1,0:T(8,128)} %get-tuple-element.308, s32[256]{0:T(256)S(1)} %bitcast.104, f32[256,64,64]{2,1,0:T(8,128)} %broadcast_multiply_fusion.2), kind=kCustom, calls=%fused_computation.7.clone.1 | custom fusion | flops 1048576 | bytes 12583936 | tf_op jit(solution)/shard_map/while/body/eval_jaxpr/scatter-add | solution.py:71
  694.9 9.0 broadcast_multiply_fusion.2
  703.9 39.4 %scatter_fusion = f32[256,64,64]{2,1,0:T(8,128)} fusion(f32[256,64,64]{2,1,0:T(8,128)} %get-tuple-element.308, s32[256]{0:T(256)S(1)} %bitcast.104, f32[256,64,64]{2,1,0:T(8,128)} %broadcast_multiply_fusion.2), kind=kCustom, calls=%fused_computation.7.clone.1 | custom fusion | flops 1048576 | bytes 12583936 | tf_op jit(solution)/shard_map/while/body/eval_jaxpr/scatter-add | solution.py:71
  753.7 9.0 broadcast_multiply_fusion.2
  762.8 39.3 %scatter_fusion = f32[256,64,64]{2,1,0:T(8,128)} fusion(f32[256,64,64]{2,1,0:T(8,128)} %get-tuple-element.308, s32[256]{0:T(256)S(1)} %bitcast.104, f32[256,64,64]{2,1,0:T(8,128)} %broadcast_multiply_fusion.2), kind=kCustom, calls=%fused_computation.7.clone.1 | custom fusion | flops 1048576 | bytes 12583936 | tf_op jit(solution)/shard_map/while/body/eval_jaxpr/scatter-add | solution.py:71
  812.4 9.0 broadcast_multiply_fusion.2
  821.4 39.4 %scatter_fusion = f32[256,64,64]{2,1,0:T(8,128)} fusion(f32[256,64,64]{2,1,0:T(8,128)} %get-tuple-element.308, s32[256]{0:T(256)S(1)} %bitcast.104, f32[256,64,64]{2,1,0:T(8,128)} %broadcast_multiply_fusion.2), kind=kCustom, calls=%fused_computation.7.clone.1 | custom fusion | flops 1048576 | bytes 12583936 | tf_op jit(solution)/shard_map/while/body/eval_jaxpr/scatter-add | solution.py:71
  871.2 9.0 broadcast_multiply_fusion.2
  880.2 39.5 %scatter_fusion = f32[256,64,64]{2,1,0:T(8,128)} fusion(f32[256,64,64]{2,1,0:T(8,128)} %get-tuple-element.308, s32[256]{0:T(256)S(1)} %bitcast.104, f32[256,64,64]{2,1,0:T(8,128)} %broadcast_multiply_fusion.2), kind=kCustom, calls=%fused_computation.7.clone.1 | custom fusion | flops 1048576 | bytes 12583936 | tf_op jit(solution)/shard_map/while/body/eval_jaxpr/scatter-add | solution.py:71
  919.7 9.7 reshape.414
  929.4 10.8 %all-to-all-start.2 = ((f32[64,1,16384]{2,1,0:T(1,128)}), f32[64,1,16384]{2,1,0:T(1,128)}, u32[]{:S(2)}, u32[]{:S(2)}) async-start(f32[64,1,16384]{2,1,0:T(1,128)} %reshape.414), calls=%async_computation.2 | async-start | bytes 8388608 | tf_op jit(solution)/shard_map/all_to_all | solution.py:75
  942.3 53.1 %all-to-all-done.2 = f32[64,1,16384]{2,1,0:T(1,128)} async-done(((f32[64,1,16384]{2,1,0:T(1,128)}), f32[64,1,16384]{2,1,0:T(1,128)}, u32[]{:S(2)}, u32[]{:S(2)}) %all-to-all-start.2) | async-done | bytes 4194336 | tf_op jit(solution)/shard_map/all_to_all | solution.py:75
  995.9 13.7 %reduce.4 = f32[64,16384]{1,0:T(8,128)} reduce(f32[64,1,16384]{2,1,0:T(1,128)} %all-to-all-done.2, f32[]{:T(128)} %broadcast.331), dimensions={1}, to_apply=%all_to_all.15.reduce_sub_computation | reduce | bytes 8388612 | tf_op jit(solution)/shard_map/all_to_all | solution.py:75
  1009.6 7.4 reshape.415
  1017.1 26.1 %scatter_fusion.1 = f32[32,64,64]{2,1,0:T(8,128)S(1)} fusion(f32[32,64,64]{2,1,0:T(8,128)S(1)} %broadcast_in_dim.9, s32[256]{0:T(256)S(1)} %bitcast.109, f32[256,64,64]{2,1,0:T(8,128)} %bitcast.102), kind=kCustom, calls=%fused_computation.8 | custom fusion | flops 1048576 | bytes 12583936 | tf_op jit(solution)/shard_map/scatter-add | solution.py:83
  (109 shorter events, 98.2 us)
Async XLA Ops:
  64.8 12.1 %copy-start.3 = (s32[1,1,64,4]{2,3,1,0:T(4,128)S(1)}, s32[1,1,64,4]{2,3,1,0:T(4,128)}, u32[]{:S(2)}) copy-start(s32[1,1,64,4]{2,3,1,0:T(4,128)} %param.11) | copy-start | bytes 3076
  64.8 268.3 %all-to-all-start = ((bf16[64,2,65536]{2,1,0:T(2,128)(2,1)}), bf16[64,2,65536]{2,1,0:T(2,128)(2,1)}, u32[]{:S(2)}, u32[]{:S(2)}) async-start(bf16[64,2,65536]{2,1,0:T(2,128)(2,1)} %reshape.412), calls=%async_computation | async-start | bytes 33554432 | tf_op jit(solution)/shard_map/all_to_all | solution.py:16
  333.1 596.3 %all-to-all-start.1 = ((s32[64,1,4]{2,1,0:T(1,128)}), s32[64,1,4]{2,1,0:T(1,128)}, u32[]{:S(2)}, u32[]{:S(2)}) async-start(s32[64,1,4]{2,1,0:T(1,128)} %bitcast.14), calls=%async_computation.1 | async-start | bytes 65536 | tf_op jit(solution)/shard_map/all_to_all | solution.py:14
  424.9 5.0 copy-start
  562.7 4.3 copy-start.2
  929.4 66.0 %all-to-all-start.2 = ((f32[64,1,16384]{2,1,0:T(1,128)}), f32[64,1,16384]{2,1,0:T(1,128)}, u32[]{:S(2)}, u32[]{:S(2)}) async-start(f32[64,1,16384]{2,1,0:T(1,128)} %reshape.414), calls=%async_computation.2 | async-start | bytes 8388608 | tf_op jit(solution)/shard_map/all_to_all | solution.py:75
  1043.3 1.0 copy-start.1
